TPU v7x, 128 devices: a whole 4x4x4 slice. The times are simulated.
128 devices in a mesh: dp: 8 (over y_hi, x), seq: 16 (over y_lo, z, core).
Axes of the slice: x: 4, y: 4 (y_hi: 2, y_lo: 2; y = y_hi * 2 + y_lo), z: 4, core: 2. Of those that a mesh axis runs over, the one named last changes fastest.
Arguments:
- tokens: bfloat16 [8, 128, 128, 1024], P('dp', 'seq'), may hold values from -12 to 12
- lengths: int32 [8], P('dp'), may hold values from 8192 to 16384, as said below
- w_qkv: bfloat16 [3, 1024, 1024], replicated, may hold values from -0.1875 to 0.1875
- out_grad: bfloat16 [8, 128, 128, 1024], P('dp', 'seq'), may hold values from -6 to 6
Outputs:
- attention: bfloat16 [8, 128, 128, 1024], P('dp', 'seq')
- input_grad: bfloat16 [8, 128, 128, 1024], P('dp', 'seq')
- w_grads: float32 [3, 1024, 1024], P(None, 'seq', 'dp')
Inputs may be any that keep to these rules, and one draw needn't show every extreme that they name: Samples at positions from lengths on are padding; some sequence is full and some has exactly 8192 valid samples.
All inputs are finite; a program needn't handle non-finite values.
Results may differ from a plain program's by a relative error of at most 0.04.
The roundings to bfloat16 on the way count: a program that leaves them out, or rounds other values in their place, can miss the bound.
Values may be sent and summed in bfloat16 or wider, within the bound.
A program may use at most 192 MiB of HBM per device.

v0:
```python
import math

import jax
import jax.numpy as jnp
from jax import lax
from jax.sharding import PartitionSpec as P

HEADS = 8


ROW_FORMS = ("srqhe,srkhe->srqhk", "srqhk,srkhe->srqhe", "srqhk,srqhe->srkhe")
COLUMN_FORMS = ("sqche,skche->sqchk", "sqchk,skche->sqche", "sqchk,sqche->skche")


def to_heads(values):
    return values.reshape(values.shape[:-1] + (HEADS, values.shape[-1] // HEADS))


def from_heads(values):
    return values.reshape(values.shape[:-2] + (values.shape[-2] * values.shape[-1],))


def project(inputs, w_qkv):
    stacked = jnp.einsum(
        "srcd,jdf->jsrcf", inputs, w_qkv, preferred_element_type=jnp.float32
    ).astype(jnp.bfloat16)
    return (to_heads(stacked[0]), to_heads(stacked[1]), to_heads(stacked[2]))


def partial_attend(query_h, key_h, value_h, allowed, forms):
    scaling = 1.0 / math.sqrt(query_h.shape[-1])
    scores = jnp.einsum(forms[0], query_h, key_h, preferred_element_type=jnp.float32) * scaling
    scores = jnp.where(allowed, scores, -1e30)
    highest = jnp.max(scores, axis=-1)
    weights = jnp.where(allowed, jnp.exp(scores - highest[..., None]), 0.0)
    totals = jnp.sum(weights, axis=-1)
    mixed = jnp.einsum(
        forms[1], weights.astype(jnp.bfloat16), value_h, preferred_element_type=jnp.float32
    )
    return (highest, totals, mixed)


def partial_back(query_h, key_h, value_h, grad_h, allowed, log_total, delta, forms):
    scaling = 1.0 / math.sqrt(query_h.shape[-1])
    scores = jnp.einsum(forms[0], query_h, key_h, preferred_element_type=jnp.float32) * scaling
    scores = jnp.where(allowed, scores, -1e30)
    weights = jnp.where(allowed, jnp.exp(scores - log_total[..., None]), 0.0)
    grad_weights = jnp.einsum(forms[0], grad_h, value_h, preferred_element_type=jnp.float32)
    grad_scores = (weights * (grad_weights - delta[..., None])).astype(jnp.bfloat16)
    grad_value = jnp.einsum(
        forms[2], weights.astype(jnp.bfloat16), grad_h, preferred_element_type=jnp.float32
    ).astype(jnp.bfloat16)
    grad_query = (
        jnp.einsum(forms[1], grad_scores, key_h, preferred_element_type=jnp.float32) * scaling
    ).astype(jnp.bfloat16)
    grad_key = (
        jnp.einsum(forms[2], grad_scores, query_h, preferred_element_type=jnp.float32) * scaling
    ).astype(jnp.bfloat16)
    return (grad_query, grad_key, grad_value)


def input_terms(grads, w_qkv):
    stacked = jnp.stack([from_heads(item) for item in grads])
    return jnp.einsum("jsrcf,jdf->srcd", stacked, w_qkv, preferred_element_type=jnp.float32)


def weight_terms(inputs, grads):
    stacked = jnp.stack([from_heads(item) for item in grads])
    return jnp.einsum("srcd,jsrcf->jdf", inputs, stacked, preferred_element_type=jnp.float32)


def body(tokens, lengths, w_qkv, out_grad):
    seq_count = lax.axis_size("seq")
    seq_index = lax.axis_index("seq")
    seq_local, row_local, columns, width = tokens.shape
    col_local = columns // seq_count
    all_rows = row_local * seq_count
    limit = lengths[:, None, None, None]
    row_ids = seq_index * row_local + jnp.arange(row_local, dtype=jnp.int32)
    col_ids = jnp.arange(columns, dtype=jnp.int32)
    key_pos = row_ids[:, None, None] * columns + col_ids[None, None, :]
    same_col = col_ids[None, None, :] == col_ids[None, :, None]
    causal_cols = col_ids[None, None, :] <= col_ids[None, :, None]
    row_allowed = causal_cols[None] & ((key_pos[None] < limit) | same_col[None])
    row_allowed = row_allowed[:, :, :, None, :]
    every_row = jnp.arange(all_rows, dtype=jnp.int32)
    own_cols = seq_index * col_local + jnp.arange(col_local, dtype=jnp.int32)
    causal_rows = every_row[None, None, :] < every_row[:, None, None]
    col_key_pos = every_row[None, None, :] * columns + own_cols[None, :, None]
    column_allowed = causal_rows[None] & (col_key_pos[None] < limit)
    column_allowed = column_allowed[:, :, :, None, :]
    query_r, key_r, value_r = project(tokens, w_qkv)
    row_high, row_total, row_mixed = partial_attend(query_r, key_r, value_r, row_allowed, ROW_FORMS)
    query_c, key_c, value_c = (
        lax.all_to_all(query_r, "seq", split_axis=2, concat_axis=1, tiled=True),
        lax.all_to_all(key_r, "seq", split_axis=2, concat_axis=1, tiled=True),
        lax.all_to_all(value_r, "seq", split_axis=2, concat_axis=1, tiled=True),
    )
    col_high_c, col_total_c, col_mixed_c = partial_attend(
        query_c, key_c, value_c, column_allowed, COLUMN_FORMS
    )
    col_high, col_total, col_mixed = (
        lax.all_to_all(col_high_c, "seq", split_axis=1, concat_axis=2, tiled=True),
        lax.all_to_all(col_total_c, "seq", split_axis=1, concat_axis=2, tiled=True),
        lax.all_to_all(col_mixed_c, "seq", split_axis=1, concat_axis=2, tiled=True),
    )
    joint = jnp.maximum(row_high, col_high)
    row_factor = jnp.exp(row_high - joint)
    col_factor = jnp.exp(col_high - joint)
    joint_total = row_total * row_factor + col_total * col_factor
    log_total = joint + jnp.log(joint_total)
    combined = (
        row_mixed * row_factor[..., None] + col_mixed * col_factor[..., None]
    ) / joint_total[..., None]
    attention = from_heads(combined).astype(jnp.bfloat16)
    grad_h = to_heads(out_grad)
    delta = jnp.einsum(
        "srche,srche->srch", to_heads(attention), grad_h, preferred_element_type=jnp.float32
    )
    row_grads = partial_back(
        query_r, key_r, value_r, grad_h, row_allowed, log_total, delta, ROW_FORMS
    )
    grad_c = lax.all_to_all(grad_h, "seq", split_axis=2, concat_axis=1, tiled=True)
    log_total_c, delta_c = (
        lax.all_to_all(log_total, "seq", split_axis=2, concat_axis=1, tiled=True),
        lax.all_to_all(delta, "seq", split_axis=2, concat_axis=1, tiled=True),
    )
    col_grads = partial_back(
        query_c, key_c, value_c, grad_c, column_allowed, log_total_c, delta_c, COLUMN_FORMS
    )
    back_q, back_k, back_v = (
        lax.all_to_all(col_grads[0], "seq", split_axis=1, concat_axis=2, tiled=True),
        lax.all_to_all(col_grads[1], "seq", split_axis=1, concat_axis=2, tiled=True),
        lax.all_to_all(col_grads[2], "seq", split_axis=1, concat_axis=2, tiled=True),
    )
    returned = (back_q, back_k, back_v)
    input_sum = input_terms(row_grads, w_qkv) + input_terms(returned, w_qkv)
    weight_part = weight_terms(tokens, row_grads) + weight_terms(tokens, returned)
    input_grad = input_sum.astype(jnp.bfloat16)
    partial_sum = lax.psum_scatter(
        weight_part.astype(jnp.bfloat16), "seq", scatter_dimension=1, tiled=True
    )
    w_grads = lax.psum_scatter(partial_sum, "dp", scatter_dimension=2, tiled=True).astype(
        jnp.float32
    )
    return (attention, input_grad, w_grads)


def solution(mesh):
    in_specs = (P("dp", "seq", None, None), P("dp"), P(), P("dp", "seq", None, None))
    out_specs = (P("dp", "seq", None, None), P("dp", "seq", None, None), P(None, "seq", "dp"))
    return jax.shard_map(body, mesh=mesh, in_specs=in_specs, out_specs=out_specs, check_vma=False)
```

profile of v0, /device:TPU:0, one launch (start us, length us, event | category | flops | bytes accessed | tf_op | source)
XLA Modules:
  0.0 741.7 jit_solution(16331930533492681562)
XLA Ops:
  8.8 8.8 %convert_bitcast_fusion = bf16[3,1,8,128,1024]{3,4,2,0,1:T(8,128)(2,1)S(1)} fusion(bf16[3,1024,1024]{2,1,0:T(8,128)(2,1)} %param.6, bf16[1,8,128,1024]{3,2,1,0:T(8,128)(2,1)S(1)} %copy-done), kind=kOutput, calls=%fused_computation.11 | convolution fusion | flops 6445596672 | bytes 14680064 | tf_op jit(solution)/shard_map/srcd,jdf->jsrcf/dot_general | solution.py:24
  20.4 4.1 copy.148
  24.5 6.6 all-to-all-start
  31.1 4.1 copy.151
  35.3 24.7 %all-to-all-done = bf16[1,8,128,8,128]{4,3,1,0,2:T(8,128)(2,1)} async-done(((bf16[1,8,128,8,128]{4,3,1,0,2:T(8,128)(2,1)}), bf16[1,8,128,8,128]{4,3,1,0,2:T(8,128)(2,1)}, u32[]{:S(2)}, u32[]{:S(2)}) %all-to-all-start) | async-done | bytes 2097184 | tf_op jit(solution)/shard_map/all_to_all | solution.py:96
  59.9 5.6 all-to-all-start.1
  65.5 4.2 copy.157
  69.7 24.6 %all-to-all-done.1 = bf16[1,8,128,8,128]{4,3,1,0,2:T(8,128)(2,1)} async-done(((bf16[1,8,128,8,128]{4,3,1,0,2:T(8,128)(2,1)}), bf16[1,8,128,8,128]{4,3,1,0,2:T(8,128)(2,1)}, u32[]{:S(2)}, u32[]{:S(2)}) %all-to-all-start.1) | async-done | bytes 2097184 | tf_op jit(solution)/shard_map/all_to_all | solution.py:95
  94.3 5.6 all-to-all-start.3
  113.5 15.2 %all-to-all-done.3 = bf16[1,8,128,8,128]{4,3,1,0,2:T(8,128)(2,1)} async-done(((bf16[1,8,128,8,128]{4,3,1,0,2:T(8,128)(2,1)}), bf16[1,8,128,8,128]{4,3,1,0,2:T(8,128)(2,1)}, u32[]{:S(2)}, u32[]{:S(2)}) %all-to-all-start.3) | async-done | bytes 2097184 | tf_op jit(solution)/shard_map/all_to_all | solution.py:97
  128.7 6.0 all-to-all-start.5
  135.8 4.9 all-to-all-done.5
  150.3 5.2 all-to-all-start.7
  176.5 7.8 %all-to-all-done.7 = bf16[1,8,128,8,128]{4,3,1,0,2:T(8,128)(2,1)} async-done(((bf16[1,8,128,8,128]{4,3,1,0,2:T(8,128)(2,1)}), bf16[1,8,128,8,128]{4,3,1,0,2:T(8,128)(2,1)}, u32[]{:S(2)}, u32[]{:S(2)}) %all-to-all-start.7) | async-done | bytes 2097184 | tf_op jit(solution)/shard_map/all_to_all | solution.py:123
  184.3 5.5 all-to-all-start.6
  189.8 7.2 convolution_bitcast_fusion
  197.1 5.4 copy.162
  202.5 6.0 all-to-all-start.4
  215.1 49.6 %all-to-all-done.4 = f32[1,128,8,8,128]{4,3,2,0,1:T(8,128)} async-done(((f32[1,128,8,8,128]{4,3,2,0,1:T(8,128)}), f32[1,128,8,8,128]{4,3,2,0,1:T(8,128)}, u32[]{:S(2)}, u32[]{:S(2)}) %all-to-all-start.4) | async-done | bytes 4194336 | tf_op jit(solution)/shard_map/all_to_all | solution.py:105
  264.7 4.7 copy.163
  269.4 5.4 copy.164
  274.8 8.8 %bitcast_convert_fusion = (f32[8,128,8,128]{1,3,2,0:T(8,128)}, bf16[1,8,128,8,128]{2,4,3,1,0:T(8,128)(2,1)}) fusion(f32[8,128,8]{1,2,0:T(8,128)S(1)} %copy-done.15, f32[1,8,128,8,128]{2,4,3,1,0:T(8,128)} %copy.164, f32[8,128,8]{1,2,0:T(8,128)S(1)} %copy-done.17, f32[8,128,8]{1,2,0:T(8,128)S(1)} %copy-done.16, bf16[8,128,8,128]{1,3,2,0:T(8,128)(2,1)} %bitcast.393, ...), kind=kOutput, calls=%fused_computation.60 | convolution fusion | flops 279969792 | bytes 17039360 | tf_op jit(solution)/shard_map/srqhk,srkhe->srqhe/dot_general | solution.py:37
  283.6 5.3 copy.213
  288.9 4.1 multiply_reduce_fusion
  294.2 10.8 %all-to-all-start.8 = ((f32[16,1,512]{2,1,0:T(1,128)}), f32[16,1,512]{2,1,0:T(1,128)S(1)}, u32[]{:S(2)}, u32[]{:S(2)}) async-start(f32[16,1,512]{2,1,0:T(1,128)} %reshape.537), calls=%async_computation.8 | async-start | bytes 65536 | tf_op jit(solution)/shard_map/all_to_all | solution.py:126
  305.0 5.3 convert_bitcast_fusion.1
  313.1 6.2 all-to-all-start.11
  323.2 7.4 fusion.9
  335.3 4.2 copy.191
  339.5 8.5 %all-to-all-done.11 = bf16[1,128,8,8,128]{4,3,2,0,1:T(8,128)(2,1)} async-done(((bf16[1,128,8,8,128]{4,3,2,0,1:T(8,128)(2,1)}), bf16[1,128,8,8,128]{4,3,2,0,1:T(8,128)(2,1)}, u32[]{:S(2)}, u32[]{:S(2)}) %all-to-all-start.11) | async-done | bytes 2097184 | tf_op jit(solution)/shard_map/all_to_all | solution.py:134
  348.0 5.7 all-to-all-start.9
  353.7 4.2 copy.174
  357.8 5.8 fusion.72
  371.3 6.7 fusion.11
  381.7 4.1 copy.195
  385.8 5.7 all-to-all-start.10
  391.8 4.2 multiply_convert_fusion.3
  399.9 5.1 multiply_convert_fusion.2
  409.0 12.6 %fusion.24 = f32[3,1024,1024,1]{2,1,0,3:T(8,128)} fusion(bf16[1,1,8,128,1024]{4,3,0,2,1:T(8,128)(2,1)} %copy.177, bf16[1,1,8,128,1024]{4,3,0,2,1:T(8,128)(2,1)} %copy.176, bf16[1,1,8,128,1024]{4,3,0,2,1:T(8,128)(2,1)} %copy.175, bf16[1,8,128,1024]{3,2,1,0:T(8,128)(2,1)S(1)} %copy-done), kind=kOutput, calls=%fused_computation.41 | convolution fusion | flops 6448742400 | bytes 20971520 | tf_op jit(solution)/shard_map/srcd,jsrcf->jdf/dot_general | solution.py:69
  428.9 11.5 %fusion.1 = bf16[3,1024,1024]{1,2,0:T(8,128)(2,1)} fusion(f32[3,1024,1024,1]{2,1,0,3:T(8,128)} %fusion.24, bf16[1,1,8,128,1024]{4,3,0,2,1:T(8,128)(2,1)S(1)} %bitcast.400, bf16[1,1,8,128,1024]{4,3,0,2,1:T(8,128)(2,1)S(1)} %bitcast.405, bf16[1,1,8,128,1024]{4,3,0,2,1:T(8,128)(2,1)S(1)} %bitcast.404, bf16[1,8,128,1024]{3,2,1,0:T(8,128)(2,1)S(1)} %copy-done), kind=kOutput, calls=%fused_computation.2 | convolution fusion | flops 6455033856 | bytes 27262976 | tf_op jit(solution)/shard_map/srcd,jsrcf->jdf/dot_general | solution.py:69
  440.4 14.3 %copy.201 = bf16[3,1024,1024]{2,0,1:T(4,128)(2,1)} copy(bf16[3,1024,1024]{1,2,0:T(8,128)(2,1)} %fusion.1) | data formatting | bytes 12582912 | tf_op jit(solution)/shard_map/convert_element_type | solution.py:141
  460.6 12.0 %fusion.4 = f32[8,128,1024,1]{2,1,3,0:T(8,128)} fusion(bf16[3,1024,1024]{2,1,0:T(8,128)(2,1)} %param.6, bf16[1,1,8,128,1024]{4,3,0,2,1:T(8,128)(2,1)} %copy.177, bf16[1,1,8,128,1024]{4,3,0,2,1:T(8,128)(2,1)} %copy.176, bf16[1,1,8,128,1024]{4,3,0,2,1:T(8,128)(2,1)} %copy.175), kind=kOutput, calls=%fused_computation.7 | convolution fusion | flops 6448742400 | bytes 16777216 | tf_op jit(solution)/shard_map/jsrcf,jdf->srcd/dot_general | solution.py:64
  472.5 126.8 %all-reduce.3.cloned.1.call-done = bf16[3,1024,1024]{2,0,1:T(4,128)(2,1)} async-done(((bf16[3,1024,1024]{2,0,1:T(4,128)(2,1)}), bf16[3,1024,1024]{2,0,1:T(4,128)(2,1)}) %all-reduce.3.cloned.1.call-update) | async-done | bytes 6291472
  600.6 26.8 %copy.235 = bf16[3,64,1024]{0,1,2:T(8,128)(2,1)} copy(bf16[3,64,1024]{2,0,1:T(4,128)(2,1)S(1)} %constant_dynamic-slice_fusion) | data formatting | bytes 786432
  627.5 25.6 %reshape.528 = bf16[1024,192]{1,0:T(8,128)(2,1)} reshape(bf16[1024,64,3]{2,1,0:T(8,128)(2,1)} %bitcast.373) | data formatting | bytes 786432
  653.0 12.3 %fusion.37 = bf16[1,8,128,1024]{3,2,1,0:T(8,128)(2,1)} fusion(f32[8,128,1024,1]{2,1,3,0:T(8,128)} %fusion.4, bf16[3,1024,1024]{2,1,0:T(8,128)(2,1)} %param.6, bf16[1,1,8,128,1024]{4,3,0,2,1:T(8,128)(2,1)} %bitcast.399, bf16[1,1,8,128,1024]{4,3,0,2,1:T(8,128)(2,1)} %bitcast.406, bf16[1,1,8,128,1024]{4,3,0,2,1:T(8,128)(2,1)} %bitcast.403), kind=kOutput, calls=%fused_computation.51 | convolution fusion | flops 6450839552 | bytes 18874368 | tf_op jit(solution)/shard_map/jsrcf,jdf->srcd/dot_general | solution.py:64
  665.3 58.7 %reduce-scatter.4.cloned.1.call-done = bf16[128,192]{1,0:T(8,128)(2,1)} async-done(((bf16[1024,192]{1,0:T(8,128)(2,1)}), bf16[128,192]{1,0:T(8,128)(2,1)}) %reduce-scatter.4.cloned.1.call-update) | async-done | bytes 49168
  724.0 6.2 reshape.529
  (116 shorter events, 105.6 us)
Async XLA Ops:
  7.2 1.6 copy-start
  24.5 35.4 %all-to-all-start = ((bf16[1,8,128,8,128]{4,3,1,0,2:T(8,128)(2,1)}), bf16[1,8,128,8,128]{4,3,1,0,2:T(8,128)(2,1)}, u32[]{:S(2)}, u32[]{:S(2)}) async-start(bf16[1,8,128,8,128]{4,3,1,0,2:T(8,128)(2,1)} %copy.148), calls=%async_computation | async-start | bytes 4194304 | tf_op jit(solution)/shard_map/all_to_all | solution.py:96
  59.9 34.4 %all-to-all-start.1 = ((bf16[1,8,128,8,128]{4,3,1,0,2:T(8,128)(2,1)}), bf16[1,8,128,8,128]{4,3,1,0,2:T(8,128)(2,1)}, u32[]{:S(2)}, u32[]{:S(2)}) async-start(bf16[1,8,128,8,128]{4,3,1,0,2:T(8,128)(2,1)} %copy.151), calls=%async_computation.1 | async-start | bytes 4194304 | tf_op jit(solution)/shard_map/all_to_all | solution.py:95
  94.3 34.4 %all-to-all-start.3 = ((bf16[1,8,128,8,128]{4,3,1,0,2:T(8,128)(2,1)}), bf16[1,8,128,8,128]{4,3,1,0,2:T(8,128)(2,1)}, u32[]{:S(2)}, u32[]{:S(2)}) async-start(bf16[1,8,128,8,128]{4,3,1,0,2:T(8,128)(2,1)} %copy.157), calls=%async_computation.3 | async-start | bytes 4194304 | tf_op jit(solution)/shard_map/all_to_all | solution.py:97
  102.9 6.3 copy-start.8
  105.6 3.6 copy-start.6
  109.2 2.0 copy-start.3
  128.7 12.1 %all-to-all-start.5 = ((f32[16,1,512]{2,1,0:T(1,128)}), f32[16,1,512]{2,1,0:T(1,128)S(1)}, u32[]{:S(2)}, u32[]{:S(2)}) async-start(f32[16,1,512]{2,1,0:T(1,128)} %reshape.533), calls=%async_computation.5 | async-start | bytes 65536 | tf_op jit(solution)/shard_map/all_to_all | solution.py:104
  140.8 9.5 %all-to-all-start.2 = ((f32[16,1,512]{2,1,0:T(1,128)}), f32[16,1,512]{2,1,0:T(1,128)S(1)}, u32[]{:S(2)}, u32[]{:S(2)}) async-start(f32[16,1,512]{2,1,0:T(1,128)} %reshape.531), calls=%async_computation.2 | async-start | bytes 65536 | tf_op jit(solution)/shard_map/all_to_all | solution.py:103
  146.5 1.3 copy-start.1
  150.3 5.5 copy-start.13
  150.3 34.0 %all-to-all-start.7 = ((bf16[1,8,128,8,128]{4,3,1,0,2:T(8,128)(2,1)}), bf16[1,8,128,8,128]{4,3,1,0,2:T(8,128)(2,1)}, u32[]{:S(2)}, u32[]{:S(2)}) async-start(bf16[1,8,128,8,128]{4,3,1,0,2:T(8,128)(2,1)} %copy.233), calls=%async_computation.7 | async-start | bytes 4194304 | tf_op jit(solution)/shard_map/all_to_all | solution.py:123
  159.1 3.4 copy-start.2
  184.3 18.2 %all-to-all-start.6 = ((f32[16,1,512]{2,1,0:T(1,128)}), f32[16,1,512]{2,1,0:T(1,128)S(1)}, u32[]{:S(2)}, u32[]{:S(2)}) async-start(f32[16,1,512]{2,1,0:T(1,128)} %reshape.535), calls=%async_computation.6 | async-start | bytes 65536 | tf_op jit(solution)/shard_map/all_to_all | solution.py:125
  202.5 62.2 %all-to-all-start.4 = ((f32[1,128,8,8,128]{4,3,2,0,1:T(8,128)}), f32[1,128,8,8,128]{4,3,2,0,1:T(8,128)}, u32[]{:S(2)}, u32[]{:S(2)}) async-start(f32[1,128,8,8,128]{4,3,2,0,1:T(8,128)} %copy.162), calls=%async_computation.4 | async-start | bytes 8388608 | tf_op jit(solution)/shard_map/all_to_all | solution.py:105
  269.4 5.4 copy-start.15
  269.4 5.4 copy-start.16
  269.4 5.4 copy-start.17
  294.2 18.9 %all-to-all-start.8 = ((f32[16,1,512]{2,1,0:T(1,128)}), f32[16,1,512]{2,1,0:T(1,128)S(1)}, u32[]{:S(2)}, u32[]{:S(2)}) async-start(f32[16,1,512]{2,1,0:T(1,128)} %reshape.537), calls=%async_computation.8 | async-start | bytes 65536 | tf_op jit(solution)/shard_map/all_to_all | solution.py:126
  313.1 34.9 %all-to-all-start.11 = ((bf16[1,128,8,8,128]{4,3,2,0,1:T(8,128)(2,1)}), bf16[1,128,8,8,128]{4,3,2,0,1:T(8,128)(2,1)}, u32[]{:S(2)}, u32[]{:S(2)}) async-start(bf16[1,128,8,8,128]{4,3,2,0,1:T(8,128)(2,1)} %copy.197), calls=%async_computation.11 | async-start | bytes 4194304 | tf_op jit(solution)/shard_map/all_to_all | solution.py:134
  323.2 8.8 %copy-start.9 = (bf16[1,8,128,8,128]{4,3,2,1,0:T(8,128)(2,1)S(1)}, bf16[1,8,128,8,128]{4,3,2,1,0:T(8,128)(2,1)}, u32[]{:S(2)}) copy-start(bf16[1,8,128,8,128]{4,3,2,1,0:T(8,128)(2,1)} %copy-done.8) | copy-start | bytes 6291460
  330.6 1.3 copy-start.4
  339.5 18.3 %copy-start.14 = (f32[8,128,8]{1,2,0:T(8,128)S(1)}, f32[8,128,8]{1,2,0:T(8,128)}, u32[]{:S(2)}) copy-start(f32[8,128,8]{1,2,0:T(8,128)} %get-tuple-element.15) | copy-start | bytes 98308
  348.0 37.8 %all-to-all-start.9 = ((bf16[1,128,8,8,128]{4,3,2,0,1:T(8,128)(2,1)}), bf16[1,128,8,8,128]{4,3,2,0,1:T(8,128)(2,1)}, u32[]{:S(2)}, u32[]{:S(2)}) async-start(bf16[1,128,8,8,128]{4,3,2,0,1:T(8,128)(2,1)} %copy.191), calls=%async_computation.9 | async-start | bytes 4194304 | tf_op jit(solution)/shard_map/all_to_all | solution.py:132
  371.3 6.7 copy-start.5
  371.3 6.7 copy-start.7
  385.8 39.3 %all-to-all-start.10 = ((bf16[1,128,8,8,128]{4,3,2,0,1:T(8,128)(2,1)}), bf16[1,128,8,8,128]{4,3,2,0,1:T(8,128)(2,1)}, u32[]{:S(2)}, u32[]{:S(2)}) async-start(bf16[1,128,8,8,128]{4,3,2,0,1:T(8,128)(2,1)} %copy.195), calls=%async_computation.10 | async-start | bytes 4194304 | tf_op jit(solution)/shard_map/all_to_all | solution.py:133
  391.5 207.9 %all-reduce.3.cloned.1.call-start = ((), (), s32[]{:S(2)}) async-start(), calls=%async_computation.14 | async-start | bytes 16777216
  425.1 3.7 copy-start.10
  425.1 3.7 copy-start.11
  427.5 1.3 copy-start.12
  454.8 0.7 copy-start.18
  454.8 269.2 %reduce-scatter.4.cloned.1.call-start = ((), (), s32[]{:S(2)}) async-start(), calls=%async_computation.13 | async-start | bytes 589824
Sparse Core Ops, SparseCore 0:
  454.9 144.4 all-reduce.2
  653.2 70.8 reduce-scatter.3
where the time goes:
time: 753 us; the launch traced here: 742 us
  waiting for transfers between devices  321 us (43%)
  local copies, waits for them, and re-layouts  198 us (26%)
  matrix products  122 us (16%)
  starting transfers between devices  72.6 us (10%)
  between operations  16.1 us (2%)
  other arithmetic  12.4 us (2%)
    unnamed x4, waiting for transfers between devices  186 us
    unnamed x56, local copies, waits for them, and re-layouts  90.1 us
    all_to_all x1, waiting for transfers between devices, body(): lax.all_to_all(col_mixed_c, 'seq', split_axis=1, concat_axis=2, tiled=True)  49.6 us
    all_to_all x1, waiting for transfers between devices, body(): lax.all_to_all(key_r, 'seq', split_axis=2, concat_axis=1, tiled=True)  24.7 us
    all_to_all x1, waiting for transfers between devices, body(): lax.all_to_all(query_r, 'seq', split_axis=2, concat_axis=1, tiled=True)  24.6 us
    dot_general x2, matrix products, input_terms(): jnp.einsum('jsrcf,jdf->srcd', stacked, w_qkv, preferred_element_type=jnp....  24.3 us
    dot_general x2, matrix products, weight_terms(): jnp.einsum('srcd,jsrcf->jdf', inputs, stacked, preferred_element_type=jnp...  24.1 us
    dot_general x2, matrix products, partial_attend(): jnp.einsum(forms[1], weights.astype(jnp.bfloat16), value_h, preferred_ele...  16 us
  transfers between devices with their start and end apart: 14, of which 10 were waited for; matrix products, arithmetic and copies ran while one was open for 25% of the time, Pallas kernels for 0%

commit v1 on v0

v1 whole, which is shorter than its diff:
```python
import math

import jax
import jax.numpy as jnp
from jax import lax
from jax.experimental import pallas as pl
from jax.experimental.pallas import tpu as pltpu
from jax.sharding import PartitionSpec as P

BF = jnp.bfloat16
F32 = jnp.float32
SCALE = 1.0 / math.sqrt(128.0)
HEADS = 8
NT_W = 512
MESH = pl.DeviceIdType.MESH


def nt(a, b):
    return lax.dot_general(a, b, (((1,), (1,)), ((), ())), preferred_element_type=F32)


def tn(a, b):
    return lax.dot_general(a, b, (((0,), (0,)), ((), ())), preferred_element_type=F32)


def nn(a, b):
    return jnp.dot(a, b, preferred_element_type=F32)


def cols(h):
    return slice(h * 128, h * 128 + 128)


def tile(t, width):
    return pl.ds(pl.multiple_of(t * width, width), width)


def allowed(side, index, length):
    key = lax.broadcasted_iota(jnp.int32, (128, 128), 0)
    query = lax.broadcasted_iota(jnp.int32, (128, 128), 1)
    if side == 0:
        return (key <= query) & ((index * 128 + key < length) | (key == query))
    return (key < query) & (key * 128 + index < length)


def pipelined(count, gap, first, second, third):
    for h in range(count + 2 * gap):
        if h < count:
            first(h)
        if 0 <= h - gap < count:
            second(h - gap)
        if 0 <= h - 2 * gap < count:
            third(h - 2 * gap)


def project(x_ref, w_ref, qkv, side, j):
    @pl.loop(0, 1024 // NT_W)
    def _(t):
        out = nn(x_ref[...].reshape(1024, 1024), w_ref[j, :, tile(t, NT_W)])
        qkv[j, side * 8 : side * 8 + 8, :, tile(t, NT_W)] = out.astype(BF).reshape(8, 128, NT_W)


def attend(qkv, g_ref, stats, side, me, length, store):
    @pl.loop(0, 8)
    def _(i):
        at = side * 8 + i
        mask = allowed(side, me * 8 + i, length)
        scores, weights = {}, {}

        def first(h):
            value = qkv[2, at, :, cols(h)]
            scores[h] = (nt(qkv[1, at, :, cols(h)], qkv[0, at, :, cols(h)]), nt(value, g_ref[i, :, cols(h)]))

        def second(h):
            score, grad = scores.pop(h)
            score = jnp.where(mask, score * SCALE, -1e30)
            highest = jnp.max(score, axis=0, keepdims=True)
            weight = jnp.exp(score - jnp.maximum(highest, -1e29))
            row = pl.ds(i * 8 + h, 1)
            stats[side, 0, row, :] = highest
            stats[side, 1, row, :] = jnp.sum(weight, axis=0, keepdims=True)
            stats[side, 2, row, :] = jnp.sum(weight * grad, axis=0, keepdims=True)
            weights[h] = weight.astype(BF)

        def third(h):
            store(i, h, tn(weights.pop(h), qkv[2, at, :, cols(h)]))

        pipelined(HEADS, 2, first, second, third)


def attend_back(qkv, g_ref, joint, side, me, length):
    @pl.loop(0, 8)
    def _(i):
        at = side * 8 + i
        mask = allowed(side, me * 8 + i, length)
        scores, probs = {}, {}

        def first(h):
            scores[h] = (
                nt(qkv[1, at, :, cols(h)], qkv[0, at, :, cols(h)]),
                nt(qkv[2, at, :, cols(h)], g_ref[i, :, cols(h)]),
            )

        def second(h):
            score, grad = scores.pop(h)
            row = pl.ds(i * 8 + h, 1)
            prob = jnp.where(mask, jnp.exp(score * SCALE - joint[side, 0, row, :]), 0.0)
            probs[h] = (prob.astype(BF), (prob * (grad - joint[side, 1, row, :])).astype(BF))

        def third(h):
            prob, grad_score = probs.pop(h)
            grad_value = nn(prob, g_ref[i, :, cols(h)])
            grad_key = nn(grad_score, qkv[0, at, :, cols(h)]) * SCALE
            grad_query = tn(grad_score, qkv[1, at, :, cols(h)]) * SCALE
            qkv[2, at, :, cols(h)] = grad_value.astype(BF)
            qkv[1, at, :, cols(h)] = grad_key.astype(BF)
            qkv[0, at, :, cols(h)] = grad_query.astype(BF)

        pipelined(HEADS, 2, first, second, third)


def regroup(raw, out):
    row = lax.broadcasted_iota(jnp.int32, (256, 256), 0)
    col = lax.broadcasted_iota(jnp.int32, (256, 256), 1)
    perm = ((row // 32 == col % 8) & ((row // 8) % 4 == col // 64) & (row % 8 == (col // 8) % 8)).astype(BF)

    @pl.loop(0, 4)
    def _(i):
        moved = nn(perm, raw[pl.ds(i * 4, 4)].reshape(256, 1024)).astype(BF)
        out[:, tile(i, 32), :] = moved.reshape(8, 32, 1024)


def transpose_into(x_ref, xt, side):
    @pl.loop(0, 8)
    def _(i):
        xt[:, pl.ds(pl.multiple_of(side * 1024 + i * 128, 128), 128)] = x_ref[i].T


def pack_stats(stats, sent, side):
    for s in range(3):
        sent[side, :, s] = stats[side, s].T.reshape(16, 8, 128)


def swap_groups(rows):
    parts = [rows[8 * o : 8 * o + 8, :] for o in range(8)]
    lane = lax.broadcasted_iota(jnp.int32, (8, 128), 1)
    for b in (1, 2, 4):
        high = (lane // b) % 2 == 1
        new = list(parts)
        for v in range(8):
            if v & b == 0:
                new[v] = jnp.where(high, pltpu.roll(parts[v | b], b, 1), parts[v])
                new[v | b] = jnp.where(high, parts[v | b], pltpu.roll(parts[v], 128 - b, 1))
        parts = new
    return jnp.concatenate(parts, axis=0)


def join_stats(stats, came, joint, side, coef=None):
    other = [swap_groups(came[side, :, s].reshape(128, 128).T[:64]) for s in range(3)]
    own = [stats[side, s, :64, :] for s in range(3)]
    top = jnp.maximum(own[0], other[0])
    own_factor = jnp.exp(own[0] - top)
    other_factor = jnp.exp(other[0] - top)
    total = own[1] * own_factor + other[1] * other_factor
    joint[side, 0] = top + jnp.log(total)
    joint[side, 1] = (own[2] * own_factor + other[2] * other_factor) / total
    if coef is not None:
        pair = jnp.concatenate([own_factor / total, other_factor / total], axis=0)
        coef[...] = pair.T


def make_kernel(dp_size, seq_size):
    def kernel(
        len_ref, tok3, tok4, g3, g4, w_hbm, att_o, dx_o, dw_o,
        x_v, g_v, w_v, raw_x, raw_g, xc, gc, qkv, mix_r, mix_c, mix_in, dxs, dx_in, xt,
        rsb, rc, r1, r2, r3, stats, sent, came, joint, coef,
        lsem, osem, own_sem, ss, rs, cs, cr, ts, tr,
    ):
        dp = lax.axis_index("dp")
        me = lax.axis_index("seq")
        core = me % 2
        z = (me // 2) % 4
        ylo = me // 8
        x = dp % 4
        yhi = dp // 4
        y = yhi * 2 + ylo
        length = len_ref[0]

        def along(axis, k):
            if axis == "x":
                c = (x + k) % 4
                return (yhi * 4 + c, me), c
            if axis == "y":
                c = (y + k) % 4
                return ((c // 2) * 4 + x, (c % 2) * 8 + z * 2 + core), c
            c = (z + k) % 4
            return (dp, ylo * 8 + c * 2 + core), c

        here = {"x": x, "y": y, "z": z}

        loads = [pltpu.make_async_copy(w_hbm.at[j], w_v.at[j], lsem.at[j]) for j in range(3)]
        loads.append(pltpu.make_async_copy(tok3, x_v, lsem.at[3]))
        loads.append(pltpu.make_async_copy(g3, g_v, lsem.at[4]))
        for at in (3, 0, 4, 1, 2):
            loads[at].start()

        barrier = pltpu.get_barrier_semaphore()

        @pl.loop(1, 16)
        def _(k):
            pl.semaphore_signal(barrier, inc=1, device_id=(dp, (me + k) % 16), device_id_type=MESH)

        for k in (1, 2, 3):
            pl.semaphore_signal(barrier, inc=1, device_id=along("x", k)[0], device_id_type=MESH)
        for c in (0, 1):
            pl.semaphore_signal(
                barrier, inc=1, device_id=((1 - yhi) * 4 + x, c * 8 + z * 2 + core), device_id_type=MESH
            )
        pl.semaphore_wait(barrier, 20)

        def exchange(n, src, dst):
            def remote(k):
                p = (me + k) % 16
                return pltpu.make_async_remote_copy(
                    src(p), dst(me), ss.at[n, k], rs.at[n, k], device_id=(dp, p), device_id_type=MESH
                )

            def local():
                return pltpu.make_async_copy(src(me), dst(me), own_sem.at[n])

            def start():
                @pl.loop(1, 16)
                def _(k):
                    remote(k).start()

                local().start()

            def arrived():
                @pl.loop(1, 16)
                def _(k):
                    back = (me + 16 - k) % 16
                    pltpu.make_async_remote_copy(
                        src(back), dst(back), ss.at[n, k], rs.at[n, k], device_id=(dp, back), device_id_type=MESH
                    ).wait_recv()

                local().wait()

            def sent_all():
                @pl.loop(1, 16)
                def _(k):
                    remote(k).wait_send()

            return start, arrived, sent_all

        half = lambda t: pl.ds(t * 512, 512)
        moves = [
            exchange(0, lambda p: tok4.at[:, p], lambda p: raw_x.at[p]),
            exchange(1, lambda p: g4.at[:, p], lambda p: raw_g.at[p]),
            exchange(2, lambda p: sent.at[0, p], lambda p: came.at[1, p]),
            exchange(3, lambda p: sent.at[1, p], lambda p: came.at[0, p]),
            exchange(4, lambda p: mix_c.at[:, p], lambda p: mix_in.at[p]),
            exchange(5, lambda p: dxs.at[:, p, :, half(0)], lambda p: dx_in.at[p, :, :, half(0)]),
            exchange(6, lambda p: dxs.at[:, p, :, half(1)], lambda p: dx_in.at[p, :, :, half(1)]),
        ]
        start = [m[0] for m in moves]
        arrived = [m[1] for m in moves]

        start[0]()
        start[1]()
        stats[...] = jnp.zeros_like(stats)

        loads[3].wait()
        for j in range(3):
            loads[j].wait()
            project(x_v, w_v, qkv, 0, j)
        loads[4].wait()

        def store_row(i, h, mixed):
            mix_r[i, :, cols(h)] = mixed.astype(BF)

        attend(qkv, g_v, stats, 0, me, length, store_row)
        pack_stats(stats, sent, 0)
        start[2]()

        arrived[0]()
        regroup(raw_x, xc)
        for j in range(3):
            project(xc, w_v, qkv, 1, j)
        transpose_into(x_v, xt, 0)
        transpose_into(xc, xt, 1)
        arrived[1]()
        regroup(raw_g, gc)

        def store_column(i, h, mixed):
            mix_c[i, :, :, cols(h)] = mixed.reshape(16, 8, 128).astype(BF)

        attend(qkv, gc, stats, 1, me, length, store_column)
        pack_stats(stats, sent, 1)
        start[3]()
        start[4]()

        arrived[2]()
        join_stats(stats, came, joint, 1)
        attend_back(qkv, gc, joint, 1, me, length)

        def input_tile(side, t):
            total = None
            for j in range(3):
                grads = qkv[j, side * 8 : side * 8 + 8].reshape(1024, 1024)
                term = nt(grads, w_v[j, tile(t, 512), :])
                total = term if total is None else total + term
            return total

        for t in range(2):
            dxs[:, :, :, t * 512 : t * 512 + 512] = input_tile(1, t).reshape(8, 16, 8, 512).astype(BF)
            start[5 + t]()

        arrived[3]()
        join_stats(stats, came, joint, 0, coef)
        attend_back(qkv, g_v, joint, 0, me, length)

        order = (("x", "y", "z"), ("y", "z", "x"), ("z", "x", "y"))

        def weight_grads(j):
            @pl.loop(0, 2)
            def _(t):
                out = nn(xt[...], qkv[j, :, :, tile(t, 512)].reshape(2048, 512)).astype(BF)
                for s in range(16):
                    for b in range(4):
                        pos = {"x": b, "y": t * 2 + s // 8, "z": (s // 2) % 4}
                        a1, a2, a3 = (pos[a] for a in order[j])
                        rsb[j, s % 2, a1 * 16 + a2 * 4 + a3] = out[s * 64 : s * 64 + 64, b * 128 : b * 128 + 128]

        def core_copy(j):
            return pltpu.make_async_remote_copy(
                rsb.at[j, 1 - core], rc.at[j], cs.at[j], cr.at[j], device_id=(dp, me + 1 - 2 * core), device_id_type=MESH
            )

        def stage_copies(j, stage):
            axis = order[j][stage]
            copies = []
            for k in (1, 2, 3):
                device, c = along(axis, k)
                if stage == 0:
                    src, dst = rsb.at[j, core, pl.ds(c * 16, 16)], r1.at[j, here[axis]]
                elif stage == 1:
                    src, dst = r1.at[j, here[order[j][0]], pl.ds(c * 4, 4)], r2.at[j, here[axis]]
                else:
                    src, dst = r2.at[j, here[order[j][1]], c], r3.at[j, here[axis]]
                n = j * 3 + stage
                copies.append(
                    pltpu.make_async_remote_copy(
                        src, dst, ts.at[n, k], tr.at[n, k], device_id=device, device_id_type=MESH
                    )
                )
            return copies

        def core_sum(j):
            core_copy(j).wait_recv()

            @pl.loop(0, 4)
            def _(t):
                at = pl.ds(t * 16, 16)
                rsb[j, core, at] = (rsb[j, core, at].astype(F32) + rc[j, at].astype(F32)).astype(BF)

        def stage_start(j, stage):
            for c in stage_copies(j, stage):
                c.start()

        def stage_sum(j, stage):
            for c in stage_copies(j, stage):
                c.wait_recv()
            mine = here[order[j][stage]]
            others = [(mine + k) % 4 for k in (1, 2, 3)]
            if stage == 0:
                total = rsb[j, core, pl.ds(mine * 16, 16)].astype(F32)
                for o in others:
                    total = total + r1[j, o].astype(F32)
                r1[j, mine] = total.astype(BF)
            elif stage == 1:
                total = r1[j, here[order[j][0]], pl.ds(mine * 4, 4)].astype(F32)
                for o in others:
                    total = total + r2[j, o].astype(F32)
                r2[j, mine] = total.astype(BF)
            else:
                total = r2[j, here[order[j][1]], mine].astype(F32)
                for o in others:
                    total = total + r3[j, o].astype(F32)
                dw_o[j] = total

        weight_grads(0)
        core_copy(0).start()
        weight_grads(1)
        core_copy(1).start()
        core_sum(0)
        stage_start(0, 0)
        weight_grads(2)
        core_copy(2).start()
        core_sum(1)
        stage_start(1, 0)

        arrived[4]()
        regroup(mix_in, xc)
        core_sum(2)
        stage_start(2, 0)

        def attention_out(i):
            return pltpu.make_async_copy(mix_r.at[i], att_o.at[i], osem.at[i])

        @pl.loop(0, 8)
        def _(i):
            factors = pltpu.roll(coef[...], (128 - i * 8) % 128, 1)
            for h in range(HEADS):
                both = mix_r[i, :, cols(h)].astype(F32) * factors[:, h : h + 1]
                both = both + xc[i, :, cols(h)].astype(F32) * factors[:, 64 + h : 65 + h]
                mix_r[i, :, cols(h)] = both.astype(BF)
            attention_out(i).start()

        stage_sum(0, 0)
        stage_start(0, 1)
        arrived[5]()
        arrived[6]()
        regroup(dx_in, gc)
        stage_sum(1, 0)
        stage_start(1, 1)

        def input_out(t):
            return pltpu.make_async_copy(x_v.at[:, :, half(t)], dx_o.at[:, :, half(t)], osem.at[8 + t])

        for t in range(2):
            whole = input_tile(0, t) + gc[:, :, t * 512 : t * 512 + 512].reshape(1024, 512).astype(F32)
            x_v[:, :, t * 512 : t * 512 + 512] = whole.astype(BF).reshape(8, 128, 512)
            input_out(t).start()
            if t == 0:
                stage_sum(2, 0)
                stage_start(2, 1)
                stage_sum(0, 1)
                stage_start(0, 2)
        stage_sum(1, 1)
        stage_start(1, 2)
        stage_sum(2, 1)
        stage_start(2, 2)
        for j in range(3):
            stage_sum(j, 2)

        for m in moves:
            m[2]()
        for j in range(3):
            core_copy(j).wait_send()
            for stage in range(3):
                for c in stage_copies(j, stage):
                    c.wait_send()
        for i in range(8):
            attention_out(i).wait()
        for t in range(2):
            input_out(t).wait()

    return kernel


def body(tokens, lengths, w_qkv, out_grad):
    tok3 = tokens.reshape(8, 128, 1024)
    g3 = out_grad.reshape(8, 128, 1024)
    tok4 = tok3.reshape(8, 16, 8, 1024)
    g4 = g3.reshape(8, 16, 8, 1024)
    any_spec = pl.BlockSpec(memory_space=pl.ANY)
    vm = pltpu.VMEM
    dma = pltpu.SemaphoreType.DMA
    attention, input_grad, w_grads = pl.pallas_call(
        make_kernel(lax.axis_size("dp"), lax.axis_size("seq")),
        out_shape=(
            jax.ShapeDtypeStruct((8, 128, 1024), BF),
            jax.ShapeDtypeStruct((8, 128, 1024), BF),
            jax.ShapeDtypeStruct((3, 64, 128), F32),
        ),
        in_specs=[pl.BlockSpec(memory_space=pltpu.SMEM)] + [any_spec] * 5,
        out_specs=(any_spec, any_spec, pl.BlockSpec(memory_space=vm)),
        scratch_shapes=[
            vm((8, 128, 1024), BF),
            vm((8, 128, 1024), BF),
            vm((3, 1024, 1024), BF),
            vm((16, 8, 8, 1024), BF),
            vm((16, 8, 8, 1024), BF),
            vm((8, 128, 1024), BF),
            vm((8, 128, 1024), BF),
            vm((3, 16, 128, 1024), BF),
            vm((8, 128, 1024), BF),
            vm((8, 16, 8, 1024), BF),
            vm((16, 8, 8, 1024), BF),
            vm((8, 16, 8, 1024), BF),
            vm((16, 8, 8, 1024), BF),
            vm((1024, 2048), BF),
            vm((3, 2, 64, 64, 128), BF),
            vm((3, 64, 64, 128), BF),
            vm((3, 4, 16, 64, 128), BF),
            vm((3, 4, 4, 64, 128), BF),
            vm((3, 4, 64, 128), BF),
            vm((2, 3, 128, 128), F32),
            vm((2, 16, 3, 8, 128), F32),
            vm((2, 16, 3, 8, 128), F32),
            vm((2, 2, 64, 128), F32),
            vm((128, 128), F32),
            dma((5,)),
            dma((10,)),
            dma((7,)),
            dma((7, 16)),
            dma((7, 16)),
            dma((3,)),
            dma((3,)),
            dma((9, 4)),
            dma((9, 4)),
        ],
        compiler_params=pltpu.CompilerParams(
            collective_id=0, has_side_effects=True, vmem_limit_bytes=67043328
        ),
        name="strided_attention",
    )(lengths, tok3, tok4, g3, g4, w_qkv)
    return (attention.reshape(tokens.shape), input_grad.reshape(tokens.shape), w_grads)


def solution(mesh):
    in_specs = (P("dp", "seq", None, None), P("dp"), P(), P("dp", "seq", None, None))
    out_specs = (P("dp", "seq", None, None), P("dp", "seq", None, None), P(None, "seq", "dp"))
    return jax.shard_map(body, mesh=mesh, in_specs=in_specs, out_specs=out_specs, check_vma=False)
```

time: 753 us -> 160 us (0.21)
  the two profiles are of different devices: /device:TPU:0 before, /device:TPU:97 now
where the time goes in v1:
time: 160 us
  Pallas kernels  154 us (96%)
  local copies, waits for them, and re-layouts  5.2 us (3%)
    pallas_call x1, Pallas kernels, body(): pl.pallas_call(make_kernel(lax.axis_size('dp'), lax.axis_size('seq')), ou...  154 us
    unnamed x7, local copies, waits for them, and re-layouts  5.2 us

profile of v1, /device:TPU:97, one launch (start us, length us, event | category | flops | bytes accessed | tf_op | source)
XLA Modules:
  0.0 160.1 jit_solution(5198008434445677212)
XLA Ops:
  1.3 153.6 %strided_attention.1 = (bf16[8,128,1024]{2,1,0:T(8,128)(2,1)}, bf16[8,128,1024]{2,1,0:T(8,128)(2,1)}, f32[3,64,128]{2,1,0:T(8,128)}) custom-call(s32[1]{0:T(128)S(6)} %copy.10.len_ref, bf16[8,128,1024]{2,1,0:T(8,128)(2,1)} %bitcast.6, bf16[8,16,8,1024]{3,2,1,0:T(8,128)(2,1)} %bitcast.7, bf16[8,128,1024]{2,1,0:T(8,128)(2,1)} %bitcast.8, ...), custom_call_target="tpu_custom_call" | custom-call | tf_op jit(solution)/shard_map/strided_attention/pallas_call | solution.py:469
  154.8 0.0 copy-start
  154.9 3.2 %copy.11 = bf16[1,8,128,1024]{3,2,1,0:T(8,128)(2,1)} copy(bf16[1,8,128,1024]{3,2,1,0:T(8,128)(2,1)} %bitcast.11) | data formatting | bytes 4194304
  158.1 0.0 copy-done
  158.1 0.0 copy-start.1
  158.1 1.3 copy.12
  159.4 0.0 copy-done.1
  159.4 0.6 copy.13
Async XLA Ops:
  154.8 3.2 %copy-start = (bf16[8,128,1024]{2,1,0:T(8,128)(2,1)S(1)}, bf16[8,128,1024]{2,1,0:T(8,128)(2,1)}, u32[]{:S(2)}) copy-start(bf16[8,128,1024]{2,1,0:T(8,128)(2,1)} %get-tuple-element.7) | copy-start | bytes 6291460
  158.1 1.3 copy-start.1

commit v2 on v1

v2 whole, which is shorter than its diff:
```python
import math

import jax
import jax.numpy as jnp
from jax import lax
from jax.experimental import pallas as pl
from jax.experimental.pallas import tpu as pltpu
from jax.sharding import PartitionSpec as P

BF = jnp.bfloat16
F32 = jnp.float32
SCALE = 1.0 / math.sqrt(128.0)
HEADS = 8
NT_W = 512
MESH = pl.DeviceIdType.MESH


def nt(a, b):
    return lax.dot_general(a, b, (((1,), (1,)), ((), ())), preferred_element_type=F32)


def tn(a, b):
    return lax.dot_general(a, b, (((0,), (0,)), ((), ())), preferred_element_type=F32)


def nn(a, b):
    return jnp.dot(a, b, preferred_element_type=F32)


def cols(h):
    return slice(h * 128, h * 128 + 128)


def tile(t, width):
    return pl.ds(pl.multiple_of(t * width, width), width)


def allowed(side, index, length):
    key = lax.broadcasted_iota(jnp.int32, (128, 128), 0)
    query = lax.broadcasted_iota(jnp.int32, (128, 128), 1)
    if side == 0:
        return (key <= query) & ((index * 128 + key < length) | (key == query))
    return (key < query) & (key * 128 + index < length)


def pipelined(blocks, gap, first, second, third):
    count = len(blocks)
    for n in range(count + 2 * gap):
        if n < count:
            first(*blocks[n])
        if 0 <= n - gap < count:
            second(*blocks[n - gap])
        if 0 <= n - 2 * gap < count:
            third(*blocks[n - 2 * gap])


def project(x_ref, w_ref, qkv, j):
    @pl.loop(0, 1024 // NT_W)
    def _(t):
        out = nn(x_ref[...].reshape(1024, 1024), w_ref[j, :, tile(t, NT_W)])
        qkv[j, 0:8, :, tile(t, NT_W)] = out.astype(BF).reshape(8, 128, NT_W)


def project_group(xc, w_ref, qkv, group):
    rows = tile(group, 32)

    @pl.loop(0, 3 * (1024 // NT_W))
    def _(n):
        j, t = n // (1024 // NT_W), n % (1024 // NT_W)
        out = nn(xc[:, rows, :].reshape(256, 1024), w_ref[j, :, tile(t, NT_W)])
        qkv[j, 8:16, rows, tile(t, NT_W)] = out.astype(BF).reshape(8, 32, NT_W)


def row_stats(qkv, g_ref, stats, me, length):
    @pl.loop(0, 8)
    def _(i):
        mask = allowed(0, me * 8 + i, length)
        scores = {}

        def first(h):
            scores[h] = (
                nt(qkv[1, i, :, cols(h)], qkv[0, i, :, cols(h)]),
                nt(qkv[2, i, :, cols(h)], g_ref[i, :, cols(h)]),
            )

        def second(h):
            score, grad = scores.pop(h)
            score = jnp.where(mask, score * SCALE, -1e30)
            highest = jnp.max(score, axis=0, keepdims=True)
            weight = jnp.exp(score - highest)
            row = pl.ds(i * 8 + h, 1)
            stats[0, 0, row, :] = highest
            stats[0, 1, row, :] = jnp.sum(weight, axis=0, keepdims=True)
            stats[0, 2, row, :] = jnp.sum(weight * grad, axis=0, keepdims=True)

        pipelined([(h,) for h in range(HEADS)], 2, first, second, lambda h: None)


def column_forward(qkv, other, stats, joint, mix_c, me, length):
    @pl.loop(0, 8)
    def _(i):
        mask = allowed(1, me * 8 + i, length)
        scores, probs = {}, {}

        def first(h):
            scores[h] = nt(qkv[1, 8 + i, :, cols(h)], qkv[0, 8 + i, :, cols(h)])

        def second(h):
            row = pl.ds(i * 8 + h, 1)
            score = jnp.where(mask, scores.pop(h) * SCALE, -1e30)
            highest = jnp.max(score, axis=0, keepdims=True)
            weight = jnp.exp(score - jnp.maximum(highest, -1e29))
            total = jnp.sum(weight, axis=0, keepdims=True)
            row_highest = other[0, row, :]
            top = jnp.maximum(highest, row_highest)
            own_factor = jnp.exp(highest - top)
            row_factor = jnp.exp(row_highest - top)
            inverse = 1.0 / (total * own_factor + other[1, row, :] * row_factor)
            own_share = own_factor * inverse
            row_share = row_factor * inverse
            stats[1, 0, row, :] = highest
            stats[1, 1, row, :] = row_share
            stats[1, 2, row, :] = other[2, row, :] * row_share
            joint[1, 0, row, :] = own_share
            probs[h] = (weight * own_share).astype(BF)

        def third(h):
            mixed = tn(probs.pop(h), qkv[2, 8 + i, :, cols(h)])
            mix_c[i, :, :, cols(h)] = mixed.reshape(16, 8, 128).astype(BF)

        pipelined([(h,) for h in range(HEADS)], 2, first, second, third)


def attend_back(qkv, g_ref, stats, joint, side, me, length, heads, per_step, mix=None):
    @pl.loop(0, 8 // per_step)
    def _(step):
        index = [step * per_step + n for n in range(per_step)]
        masks = [allowed(side, me * 8 + i, length) for i in index]
        scores, probs = {}, {}

        def first(n, h):
            at = side * 8 + index[n]
            scores[n, h] = (
                nt(qkv[1, at, :, cols(h)], qkv[0, at, :, cols(h)]),
                nt(qkv[2, at, :, cols(h)], g_ref[index[n], :, cols(h)]),
            )

        def second(n, h):
            score, grad = scores.pop((n, h))
            row = pl.ds(index[n] * 8 + h, 1)
            prob = jnp.exp(score * SCALE - stats[side, 0, row, :]) * joint[side, 0, row, :]
            prob = jnp.where(masks[n], prob, 0.0)
            if side == 1:
                delta = stats[1, 2, row, :] + jnp.sum(prob * grad, axis=0, keepdims=True)
                joint[1, 1, row, :] = delta
            else:
                delta = joint[0, 1, row, :]
            probs[n, h] = (prob.astype(BF), (prob * (grad - delta)).astype(BF))

        def third(n, h):
            at = side * 8 + index[n]
            prob, grad_score = probs.pop((n, h))
            grad_value = nn(prob, g_ref[index[n], :, cols(h)])
            if mix is not None:
                mix[index[n], :, cols(h)] = tn(prob, qkv[2, at, :, cols(h)]).astype(BF)
            grad_key = nn(grad_score, qkv[0, at, :, cols(h)]) * SCALE
            grad_query = tn(grad_score, qkv[1, at, :, cols(h)]) * SCALE
            qkv[2, at, :, cols(h)] = grad_value.astype(BF)
            qkv[1, at, :, cols(h)] = grad_key.astype(BF)
            qkv[0, at, :, cols(h)] = grad_query.astype(BF)

        pipelined([(n, h) for n in range(per_step) for h in heads], 2, first, second, third)


def permutation():
    row = lax.broadcasted_iota(jnp.int32, (256, 256), 0)
    col = lax.broadcasted_iota(jnp.int32, (256, 256), 1)
    return ((row // 32 == col % 8) & ((row // 8) % 4 == col // 64) & (row % 8 == (col // 8) % 8)).astype(BF)


def regroup(raw, out, group, lanes):
    width = lanes.stop - lanes.start
    moved = nn(permutation(), raw[pl.ds(group * 4, 4), :, :, lanes].reshape(256, width))
    out[:, tile(group, 32), lanes] = moved.astype(BF).reshape(8, 32, width)


def regroup_add(raw, out, group, lanes):
    width = lanes.stop - lanes.start
    moved = nn(permutation(), raw[pl.ds(group * 4, 4), :, :, lanes].reshape(256, width)).reshape(8, 32, width)
    out[:, tile(group, 32), lanes] = (moved + out[:, tile(group, 32), lanes].astype(F32)).astype(BF)


def transpose_into(x_ref, xt, side):
    @pl.loop(0, 8)
    def _(i):
        xt[:, pl.ds(pl.multiple_of(side * 1024 + i * 128, 128), 128)] = x_ref[i].T


def swap_groups(rows):
    parts = [rows[8 * o : 8 * o + 8, :] for o in range(8)]
    lane = lax.broadcasted_iota(jnp.int32, (8, 128), 1)
    for b in (1, 2, 4):
        high = (lane // b) % 2 == 1
        new = list(parts)
        for v in range(8):
            if v & b == 0:
                new[v] = jnp.where(high, pltpu.roll(parts[v | b], b, 1), parts[v])
                new[v | b] = jnp.where(high, parts[v | b], pltpu.roll(parts[v], 128 - b, 1))
        parts = new
    return jnp.concatenate(parts, axis=0)


def pack(rows, sent, s):
    sent[:, s] = rows.T.reshape(16, 8, 128)


def unpack(came, s):
    return swap_groups(came[:, s].reshape(128, 128).T[:64])


def make_kernel(dp_size, seq_size):
    def kernel(
        len_ref, tok3, tok4, g3, g4, w_hbm, att_o, dx_o, dw_o,
        x_v, g_v, w_v, raw_x, raw_g, xc, gc, qkv, mix_r, mix_c, mix_in, dxs, dx_in, xt,
        rsb, rc, r1, r2, r3, rsb_s, rc_s, r1_s, r2_s, r3_s, stats, sent_r, came_c, sent_c, came_r, other, joint,
        lsem, osem, own_sem, ss, rs, cs, cr, ts, tr,
    ):
        dp = lax.axis_index("dp")
        me = lax.axis_index("seq")
        core = me % 2
        z = (me // 2) % 4
        ylo = me // 8
        x = dp % 4
        yhi = dp // 4
        y = yhi * 2 + ylo
        length = len_ref[0]
        large, small = (rsb, rc, r1, r2, r3), (rsb_s, rc_s, r1_s, r2_s, r3_s)

        def along(axis, k):
            if axis == "x":
                c = (x + k) % 4
                return (yhi * 4 + c, me), c
            if axis == "y":
                c = (y + k) % 4
                return ((c // 2) * 4 + x, (c % 2) * 8 + z * 2 + core), c
            c = (z + k) % 4
            return (dp, ylo * 8 + c * 2 + core), c

        here = {"x": x, "y": y, "z": z}

        loads = [pltpu.make_async_copy(w_hbm.at[j], w_v.at[j], lsem.at[j]) for j in range(3)]
        loads.append(pltpu.make_async_copy(tok3, x_v, lsem.at[3]))
        loads.append(pltpu.make_async_copy(g3, g_v, lsem.at[4]))
        for at in (3, 0, 4, 1, 2):
            loads[at].start()

        barrier = pltpu.get_barrier_semaphore()

        @pl.loop(1, 16)
        def _(k):
            pl.semaphore_signal(barrier, inc=1, device_id=(dp, (me + k) % 16), device_id_type=MESH)

        for k in (1, 2, 3):
            pl.semaphore_signal(barrier, inc=1, device_id=along("x", k)[0], device_id_type=MESH)
        for c in (0, 1):
            pl.semaphore_signal(
                barrier, inc=1, device_id=((1 - yhi) * 4 + x, c * 8 + z * 2 + core), device_id_type=MESH
            )
        pl.semaphore_wait(barrier, 20)

        def partner(dy, dz, dc):
            return ((ylo + dy) % 2) * 8 + ((z + dz) % 4) * 2 + (core + dc) % 2

        def exchange(n, src, dst):
            def copy(dy, dz, dc, slot):
                p = partner(dy, dz, dc)
                q = dy * 8 + dz * 2 + dc
                return pltpu.make_async_remote_copy(
                    src(p), dst(slot), ss.at[n, q], rs.at[n, q], device_id=(dp, p), device_id_type=MESH
                )

            def local():
                return pltpu.make_async_copy(src(me), dst(me), own_sem.at[n])

            def start():
                for dz in (0, 1, 3, 2):

                    @pl.loop(1 if dz == 0 else 0, 4)
                    def _(e):
                        copy(e // 2, dz, e % 2, me).start()

                local().start()

            def arrived_from(dy, dz, dc):
                p = partner(dy, 4 - dz, dc)
                q = dy * 8 + dz * 2 + dc
                pltpu.make_async_remote_copy(
                    src(p), dst(p), ss.at[n, q], rs.at[n, q], device_id=(dp, p), device_id_type=MESH
                ).wait_recv()

            def arrived():
                @pl.loop(1, 16)
                def _(q):
                    arrived_from(q // 8, (q // 2) % 4, q % 2)

                local().wait()

            def sent_all():
                @pl.loop(1, 16)
                def _(q):
                    copy(q // 8, (q // 2) % 4, q % 2, me).wait_send()

            return start, arrived, sent_all, arrived_from, local

        half = lambda t: pl.ds(t * 512, 512)
        lane_half = lambda t: slice(t * 512, t * 512 + 512)
        moves = [
            exchange(0, lambda p: tok4.at[:, p], lambda p: raw_x.at[p]),
            exchange(1, lambda p: sent_r.at[p], lambda p: came_c.at[p]),
            exchange(2, lambda p: g4.at[:, p, :, half(0)], lambda p: raw_g.at[p, :, :, half(0)]),
            exchange(3, lambda p: g4.at[:, p, :, half(1)], lambda p: raw_g.at[p, :, :, half(1)]),
            exchange(4, lambda p: mix_c.at[:, p, :, pl.ds(0, 256)], lambda p: mix_in.at[p, :, :, pl.ds(0, 256)]),
            exchange(5, lambda p: sent_c.at[p], lambda p: came_r.at[p]),
            exchange(6, lambda p: mix_c.at[:, p, :, pl.ds(256, 768)], lambda p: mix_in.at[p, :, :, pl.ds(256, 768)]),
            exchange(7, lambda p: dxs.at[:, p, :, half(0)], lambda p: dx_in.at[p, :, :, half(0)]),
            exchange(8, lambda p: dxs.at[:, p, :, half(1)], lambda p: dx_in.at[p, :, :, half(1)]),
        ]
        start = [m[0] for m in moves]
        arrived = [m[1] for m in moves]

        start[0]()

        loads[3].wait()
        for j in range(3):
            loads[j].wait()
            project(x_v, w_v, qkv, j)
        loads[4].wait()
        stats[...] = jnp.zeros_like(stats)
        row_stats(qkv, g_v, stats, me, length)
        for s in range(3):
            pack(stats[0, s], sent_r, s)
        start[1]()
        start[2]()
        start[3]()
        transpose_into(x_v, xt, 0)

        for n in range(4):
            for dz in (0, 3 - 2 * (z % 2)) if n < 2 else (2, 1 + 2 * (z % 2)):
                for dc in (0, 1):
                    if n == 0 and isinstance(dz, int) and dc == 0:
                        moves[0][4]().wait()
                    else:
                        moves[0][3](n % 2, dz, dc)
            group = ((ylo + n % 2) % 2) * 2 + (z // 2 + n // 2) % 2
            regroup(raw_x, xc, group, slice(0, 1024))
            project_group(xc, w_v, qkv, group)
        arrived[1]()
        for s in range(3):
            other[s] = unpack(came_c, s)
        column_forward(qkv, other, stats, joint, mix_c, me, length)
        start[4]()

        for t in range(2):
            if t == 1:
                transpose_into(xc, xt, 1)
            arrived[2 + t]()

            @pl.loop(0, 4)
            def _(i):
                regroup(raw_g, gc, i, lane_half(t))

            attend_back(qkv, gc, stats, joint, 1, me, length, range(4 * t, 4 * t + 4), 2)
        stats[1, 2, :64, :] = joint[1, 1]
        pack(stats[1, 1], sent_c, 0)
        pack(stats[1, 2], sent_c, 1)
        start[5]()
        start[6]()

        def input_tile(side, t):
            total = None
            for j in range(3):
                grads = qkv[j, side * 8 : side * 8 + 8].reshape(1024, 1024)
                term = nt(grads, w_v[j, tile(t, 512), :])
                total = term if total is None else total + term
            return total

        dxs[:, :, :, lane_half(0)] = input_tile(1, 0).reshape(8, 16, 8, 512).astype(BF)
        start[7]()

        arrived[5]()
        joint[0, 0] = unpack(came_r, 0)
        joint[0, 1] = unpack(came_r, 1)
        attend_back(qkv, g_v, stats, joint, 0, me, length, range(HEADS), 1, mix_r)

        pieces = ((0, 0, 64, "xyz"), (1, 0, 64, "xzy"), (2, 0, 32, "yzx"), (2, 32, 32, "zyx"))

        def buffers(n):
            return [ref.at[n % 2] for ref in (large if n < 2 else small)]

        def weight_grads(j):
            @pl.loop(0, 2)
            def _(t):
                out = nn(xt[...], qkv[j, :, :, tile(t, 512)].reshape(2048, 512)).astype(BF)
                for n, (of, low, rows, order) in enumerate(pieces):
                    if of != j:
                        continue
                    block = buffers(n)[0]
                    for s in range(16):
                        for b in range(4):
                            pos = {"x": b, "y": t * 2 + s // 8, "z": (s // 2) % 4}
                            a1, a2, a3 = (pos[a] for a in order)
                            first = s * 64 + low
                            block[s % 2, a1 * 16 + a2 * 4 + a3] = out[first : first + rows, b * 128 : b * 128 + 128]

        def core_copy(n):
            block, rc = buffers(n)[:2]
            return pltpu.make_async_remote_copy(
                block.at[1 - core], rc, cs.at[n], cr.at[n], device_id=(dp, me + 1 - 2 * core), device_id_type=MESH
            )

        def stage_copies(n, stage):
            order = pieces[n][3]
            block, _, r1, r2, r3 = buffers(n)
            axis = order[stage]
            copies = []
            for k in (1, 2, 3):
                device, c = along(axis, k)
                if stage == 0:
                    src, dst = block.at[core, pl.ds(c * 16, 16)], r1.at[here[axis]]
                elif stage == 1:
                    src, dst = r1.at[here[order[0]], pl.ds(c * 4, 4)], r2.at[here[axis]]
                else:
                    src, dst = r2.at[here[order[1]], c], r3.at[here[axis]]
                at = n * 3 + stage
                copies.append(
                    pltpu.make_async_remote_copy(
                        src, dst, ts.at[at, k], tr.at[at, k], device_id=device, device_id_type=MESH
                    )
                )
            return copies

        def core_sum(n):
            core_copy(n).wait_recv()
            block, rc = buffers(n)[:2]

            @pl.loop(0, 4)
            def _(t):
                at = pl.ds(t * 16, 16)
                block[core, at] = (block[core, at].astype(F32) + rc[at].astype(F32)).astype(BF)

        def stage_start(n, stage):
            for c in stage_copies(n, stage):
                c.start()

        def stage_sum(n, stage):
            for c in stage_copies(n, stage):
                c.wait_recv()
            j, low, rows, order = pieces[n]
            block, _, r1, r2, r3 = buffers(n)
            mine = here[order[stage]]
            if stage == 0:
                total, came = block[core, pl.ds(mine * 16, 16)], r1
            elif stage == 1:
                total, came = r1[here[order[0]], pl.ds(mine * 4, 4)], r2
            else:
                total, came = r2[here[order[1]], mine], r3
            total = total.astype(F32)
            for k in (1, 2, 3):
                total = total + came[(mine + k) % 4].astype(F32)
            if stage < 2:
                came[mine] = total.astype(BF)
            else:
                dw_o[j, low : low + rows] = total

        weight_grads(0)
        core_copy(0).start()
        weight_grads(1)
        core_copy(1).start()
        core_sum(0)
        stage_start(0, 0)
        dxs[:, :, :, lane_half(1)] = input_tile(1, 1).reshape(8, 16, 8, 512).astype(BF)
        start[8]()
        core_sum(1)
        stage_start(1, 0)
        weight_grads(2)
        core_copy(2).start()
        core_copy(3).start()

        arrived[4]()
        arrived[6]()

        def attention_out(i):
            return pltpu.make_async_copy(mix_r.at[:, tile(i, 32)], att_o.at[:, tile(i, 32)], osem.at[i])

        @pl.loop(0, 4)
        def _(i):
            regroup_add(mix_in, mix_r, i, slice(0, 1024))
            attention_out(i).start()

        core_sum(2)
        stage_start(2, 0)
        core_sum(3)
        stage_start(3, 0)

        def input_grads(t):
            x_v[:, :, lane_half(t)] = input_tile(0, t).astype(BF).reshape(8, 128, 512)

        def input_out(t):
            return pltpu.make_async_copy(x_v.at[:, :, half(t)], dx_o.at[:, :, half(t)], osem.at[4 + t])

        def input_sum(t):
            arrived[7 + t]()

            @pl.loop(0, 4)
            def _(i):
                regroup_add(dx_in, x_v, i, lane_half(t))

            input_out(t).start()

        input_grads(0)
        stage_sum(0, 0)
        stage_start(0, 1)
        input_grads(1)
        input_sum(0)
        for n in (1, 2, 3):
            stage_sum(n, 0)
            stage_start(n, 1)
        stage_sum(0, 1)
        stage_start(0, 2)
        input_sum(1)
        for n in (1, 2, 3):
            stage_sum(n, 1)
            stage_start(n, 2)
        for n in range(4):
            stage_sum(n, 2)

        for m in moves:
            m[2]()
        for n in range(4):
            core_copy(n).wait_send()
            for stage in range(3):
                for c in stage_copies(n, stage):
                    c.wait_send()
        for i in range(4):
            attention_out(i).wait()
        for t in range(2):
            input_out(t).wait()

    return kernel


def body(tokens, lengths, w_qkv, out_grad):
    tok3 = tokens.reshape(8, 128, 1024)
    g3 = out_grad.reshape(8, 128, 1024)
    tok4 = tok3.reshape(8, 16, 8, 1024)
    g4 = g3.reshape(8, 16, 8, 1024)
    any_spec = pl.BlockSpec(memory_space=pl.ANY)
    vm = pltpu.VMEM
    dma = pltpu.SemaphoreType.DMA
    attention, input_grad, w_grads = pl.pallas_call(
        make_kernel(lax.axis_size("dp"), lax.axis_size("seq")),
        out_shape=(
            jax.ShapeDtypeStruct((8, 128, 1024), BF),
            jax.ShapeDtypeStruct((8, 128, 1024), BF),
            jax.ShapeDtypeStruct((3, 64, 128), F32),
        ),
        in_specs=[pl.BlockSpec(memory_space=pltpu.SMEM)] + [any_spec] * 5,
        out_specs=(any_spec, any_spec, pl.BlockSpec(memory_space=vm)),
        scratch_shapes=[
            vm((8, 128, 1024), BF),
            vm((8, 128, 1024), BF),
            vm((3, 1024, 1024), BF),
            vm((16, 8, 8, 1024), BF),
            vm((16, 8, 8, 1024), BF),
            vm((8, 128, 1024), BF),
            vm((8, 128, 1024), BF),
            vm((3, 16, 128, 1024), BF),
            vm((8, 128, 1024), BF),
            vm((8, 16, 8, 1024), BF),
            vm((16, 8, 8, 1024), BF),
            vm((8, 16, 8, 1024), BF),
            vm((16, 8, 8, 1024), BF),
            vm((1024, 2048), BF),
            vm((2, 2, 64, 64, 128), BF),
            vm((2, 64, 64, 128), BF),
            vm((2, 4, 16, 64, 128), BF),
            vm((2, 4, 4, 64, 128), BF),
            vm((2, 4, 64, 128), BF),
            vm((2, 2, 64, 32, 128), BF),
            vm((2, 64, 32, 128), BF),
            vm((2, 4, 16, 32, 128), BF),
            vm((2, 4, 4, 32, 128), BF),
            vm((2, 4, 32, 128), BF),
            vm((2, 3, 128, 128), F32),
            vm((16, 3, 8, 128), F32),
            vm((16, 3, 8, 128), F32),
            vm((16, 2, 8, 128), F32),
            vm((16, 2, 8, 128), F32),
            vm((3, 64, 128), F32),
            vm((2, 2, 64, 128), F32),
            dma((5,)),
            dma((6,)),
            dma((9,)),
            dma((9, 16)),
            dma((9, 16)),
            dma((4,)),
            dma((4,)),
            dma((12, 4)),
            dma((12, 4)),
        ],
        compiler_params=pltpu.CompilerParams(
            collective_id=0, has_side_effects=True, vmem_limit_bytes=67043328
        ),
        name="strided_attention",
    )(lengths, tok3, tok4, g3, g4, w_qkv)
    return (attention.reshape(tokens.shape), input_grad.reshape(tokens.shape), w_grads)


def solution(mesh):
    in_specs = (P("dp", "seq", None, None), P("dp"), P(), P("dp", "seq", None, None))
    out_specs = (P("dp", "seq", None, None), P("dp", "seq", None, None), P(None, "seq", "dp"))
    return jax.shard_map(body, mesh=mesh, in_specs=in_specs, out_specs=out_specs, check_vma=False)
```

time: 160 us -> 137 us (0.86)
  the two profiles are of different devices: /device:TPU:97 before, /device:TPU:0 now
where the time goes in v2:
time: 137 us; the launch traced here: 136 us
  Pallas kernels  130 us (95%)
  local copies, waits for them, and re-layouts  5.2 us (4%)
    pallas_call x1, Pallas kernels, body(): pl.pallas_call(make_kernel(lax.axis_size('dp'), lax.axis_size('seq')), ou...  130 us
    unnamed x7, local copies, waits for them, and re-layouts  5.2 us

profile of v2, /device:TPU:0, one launch (start us, length us, event | category | flops | bytes accessed | tf_op | source)
XLA Modules:
  0.0 136.4 jit_solution(3078733605765972158)
XLA Ops:
  1.3 129.9 %strided_attention.1 = (bf16[8,128,1024]{2,1,0:T(8,128)(2,1)}, bf16[8,128,1024]{2,1,0:T(8,128)(2,1)}, f32[3,64,128]{2,1,0:T(8,128)}) custom-call(s32[1]{0:T(128)S(6)} %copy.10.len_ref, bf16[8,128,1024]{2,1,0:T(8,128)(2,1)} %bitcast.6, bf16[8,16,8,1024]{3,2,1,0:T(8,128)(2,1)} %bitcast.7, bf16[8,128,1024]{2,1,0:T(8,128)(2,1)} %bitcast.8, ...), custom_call_target="tpu_custom_call" | custom-call | tf_op jit(solution)/shard_map/strided_attention/pallas_call | solution.py:560
  131.2 0.0 copy-start
  131.2 3.2 %copy.11 = bf16[1,8,128,1024]{3,2,1,0:T(8,128)(2,1)} copy(bf16[1,8,128,1024]{3,2,1,0:T(8,128)(2,1)} %bitcast.11) | data formatting | bytes 4194304
  134.4 0.0 copy-done
  134.4 0.0 copy-start.1
  134.4 1.3 copy.12
  135.7 0.0 copy-done.1
  135.7 0.6 copy.13
Async XLA Ops:
  131.2 3.2 %copy-start = (bf16[8,128,1024]{2,1,0:T(8,128)(2,1)S(1)}, bf16[8,128,1024]{2,1,0:T(8,128)(2,1)}, u32[]{:S(2)}) copy-start(bf16[8,128,1024]{2,1,0:T(8,128)(2,1)} %get-tuple-element.7) | copy-start | bytes 6291460
  134.4 1.3 copy-start.1
